TPU v7x, 32 devices: a whole 2x2x4 slice. The times are simulated.
32 devices in a mesh: seq: 8 (over z, core), chan: 4 (over y, x).
Axes of the slice: x: 2, y: 2, z: 4, core: 2. Of those that a mesh axis runs over, the one named last changes fastest.
Arguments:
- gate_raw: bfloat16 [8, 2048, 2048], P('seq', None, 'chan'), may hold values from -50 to 50
- value_raw: bfloat16 [8, 2048, 2048], P('seq', None, 'chan'), may hold values from -50 to 50
- filter_gate: float32 [7, 2048], P(None, 'chan'), may hold values from -3 to 3
- filter_value: float32 [7, 2048], P(None, 'chan'), may hold values from -3 to 3
- teacher: float32 [8, 2048, 2048], P('seq', 'chan'), may hold values from -0.25 to 1, as said below
Outputs:
- grad_gate_raw: bfloat16 [8, 2048, 2048], P('seq', None, 'chan')
- grad_value_raw: bfloat16 [8, 2048, 2048], P('seq', None, 'chan')
- grad_filter_gate: float32 [7, 2048], P(None, 'chan')
- grad_filter_value: float32 [7, 2048], P(None, 'chan')
Inputs may be any that keep to these rules, and one draw needn't show every extreme that they name: teacher[s] is symmetric for each of the 8 sequences, with ones on its diagonal.
All inputs are finite; a program needn't handle non-finite values.
Results may differ from a plain program's by a relative error of at most 0.0059.
Values may be sent and summed in bfloat16 or wider, within the bound.
A program may use at most 128 MiB of HBM per device.

v0:
```python
import math

import jax
import jax.numpy as jnp
from jax import lax
from jax.sharding import PartitionSpec as P

TAPS = 7


epsilon = 1e-06


def causal_conv(signal, weights):
    length = signal.shape[1]
    padded = jnp.pad(signal, ((0, 0), (TAPS - 1, 0), (0, 0)))
    summed = jnp.zeros(signal.shape, jnp.float32)
    for tap_index in range(TAPS):
        window = padded[:, TAPS - 1 - tap_index : TAPS - 1 - tap_index + length]
        summed = summed + weights[tap_index] * window.astype(jnp.float32)
    return summed


def adjoint_conv(upstream, weights):
    length = upstream.shape[1]
    padded = jnp.pad(upstream, ((0, 0), (0, TAPS - 1), (0, 0)))
    summed = jnp.zeros(upstream.shape, jnp.float32)
    for tap_index in range(TAPS):
        summed = summed + weights[tap_index] * padded[:, tap_index : tap_index + length]
    return summed


def tap_sums(upstream, signal):
    length = signal.shape[1]
    padded = jnp.pad(signal, ((0, 0), (TAPS - 1, 0), (0, 0)))
    return jnp.stack(
        [
            jnp.sum(
                upstream
                * padded[:, TAPS - 1 - tap_index : TAPS - 1 - tap_index + length].astype(
                    jnp.float32
                ),
                axis=(0, 1),
            )
            for tap_index in range(TAPS)
        ]
    )


def gram_rows(normed, offset, stripe, teacher, factor, full_width):
    own_rows = lax.dynamic_slice_in_dim(normed, offset, stripe, 1)
    similarity = (
        jnp.einsum("srd,std->srt", own_rows, normed, preferred_element_type=jnp.float32)
        / full_width
    )
    residue = (factor * (similarity - teacher)).astype(jnp.bfloat16)
    return jnp.einsum("srt,std->srd", residue, normed, preferred_element_type=jnp.float32)


def on_device(gate_raw, value_raw, filter_gate, filter_value, teacher):
    seq_count, length, local_width = gate_raw.shape
    groups = lax.axis_size("chan")
    stripe = length // groups
    offset = lax.axis_index("chan") * stripe
    full_width = local_width * groups
    factor = 16.0 / math.sqrt(length)
    gate_conv = causal_conv(gate_raw, filter_gate)
    value_conv = causal_conv(value_raw, filter_value)
    hidden = (gate_conv * value_conv).astype(jnp.bfloat16)
    hidden_f = hidden.astype(jnp.float32)
    square_total = lax.psum(jnp.sum(hidden_f * hidden_f, axis=2), "chan")
    inv_rms = lax.rsqrt(square_total[:, :, None] / full_width + epsilon)
    normed_f = hidden_f * inv_rms
    normed = lax.all_gather(normed_f.astype(jnp.bfloat16), "chan", axis=2, tiled=True)
    row_part = gram_rows(normed, offset, stripe, teacher, factor, full_width)
    normed_grad = lax.all_to_all(row_part, "chan", split_axis=2, concat_axis=1, tiled=True)
    projection = lax.psum(jnp.sum(normed_f * normed_grad, axis=2) / full_width, "chan")
    hidden_grad = inv_rms * (normed_grad - normed_f * projection[:, :, None])
    gate_conv_grad = hidden_grad * value_conv
    value_conv_grad = hidden_grad * gate_conv
    grad_gate = adjoint_conv(gate_conv_grad, filter_gate).astype(jnp.bfloat16)
    grad_value = adjoint_conv(value_conv_grad, filter_value).astype(jnp.bfloat16)
    norm_factor = 1.0 / math.sqrt(lax.axis_size("seq") * seq_count * length)
    gate_taps, value_taps = lax.psum(
        (tap_sums(gate_conv_grad, gate_raw), tap_sums(value_conv_grad, value_raw)), "seq"
    )
    return (grad_gate, grad_value, gate_taps * norm_factor, value_taps * norm_factor)


def solution(mesh):
    placed = (
        P("seq", None, "chan"),
        P("seq", None, "chan"),
        P(None, "chan"),
        P(None, "chan"),
        P("seq", "chan", None),
    )
    return jax.shard_map(
        on_device,
        mesh=mesh,
        in_specs=placed,
        out_specs=(
            P("seq", None, "chan"),
            P("seq", None, "chan"),
            P(None, "chan"),
            P(None, "chan"),
        ),
        check_vma=False,
    )
```

profile of v0, /device:TPU:0, one launch (start us, length us, event | category | flops | bytes accessed | tf_op | source)
XLA Modules:
  0.0 296.8 jit_solution(16219476741442778253)
XLA Ops:
  7.2 0.0 all-gather.2.cloned.1.call-start
  7.2 1.0 fusion.66
  8.2 1.0 fusion.65
  9.2 18.7 %fusion.36 = (f32[2048]{0:T(1024)S(1)}, bf16[1,2048,512]{2,1,0:T(8,128)(2,1)S(1)}, f32[1,2048,512]{2,1,0:T(8,128)}, f32[1,2048,512]{2,1,0:T(8,128)}) fusion(f32[512]{0:T(512)S(1)} %bitcast.91, f32[512]{0:T(512)S(1)} %bitcast.93, f32[512]{0:T(512)S(1)} %bitcast.83, f32[512]{0:T(512)S(1)} %bitcast.85, f32[512]{0:T(512)S(1)} %bitcast.87, ...), kind=kLoop, calls=%fused_computation.66 | loop fusion | flops 47183872 | bytes 14716928 | tf_op jit(solution)/shard_map/reduce_sum | solution.py:71
  27.9 11.5 %psum.28 = f32[1,2048]{1,0:T(1,128)S(1)} all-reduce(f32[1,2048]{1,0:T(1,128)S(1)} %bitcast.80), channel_id=1, replica_groups=mesh['seq'=8,'chan'=4] {'chan'}, use_global_device_ids=true, to_apply=%region_1.2 | all-reduce | flops 2048 | bytes 16384 | tf_op jit(solution)/shard_map/psum | solution.py:71
  39.5 1.8 fusion.6
  41.3 0.0 all-gather.2.cloned.1.call-update
  41.3 86.9 %all-gather.2.cloned.1.call-done = bf16[1,2048,2048]{2,1,0:T(8,128)(2,1)} async-done(((bf16[1,2048,512]{2,1,0:T(8,128)(2,1)}), bf16[1,2048,2048]{2,1,0:T(8,128)(2,1)}) %all-gather.2.cloned.1.call-update) | async-done | bytes 8388624 | tf_op jit(solution)/shard_map/all_gather | solution.py:74
  128.1 18.4 %fusion.41 = f32[1,512,2048]{2,1,0:T(8,128)} fusion(bf16[1,2048,2048]{2,1,0:T(8,128)(2,1)} %all-gather.2.cloned.1.call-done, f32[1,512,2048]{2,1,0:T(8,128)} %param.9, s32[]{:T(128)S(6)} %select_n.3), kind=kOutput, calls=%fused_computation.73 | convolution fusion | flops 8594128896 | bytes 27262980 | tf_op jit(solution)/shard_map/srt,std->srd/dot_general | solution.py:57
  146.5 10.9 %copy.10 = f32[1,512,2048]{1,0,2:T(1,128)} copy(f32[1,512,2048]{2,1,0:T(8,128)} %fusion.41) | data formatting | bytes 8388608 | tf_op jit(solution)/shard_map/srt,std->srd/dot_general | solution.py:57
  157.4 53.7 %all_to_all.18 = f32[1,512,2048]{1,0,2:T(1,128)} all-to-all(f32[1,512,2048]{1,0,2:T(1,128)} %copy.10), channel_id=1, replica_groups=mesh['seq'=8,'chan'=4] {'chan'}, dimensions={2} | all-to-all | bytes 8388608 | tf_op jit(solution)/shard_map/all_to_all | solution.py:76
  211.1 10.9 %copy.11 = f32[1,4,512,512]{3,2,1,0:T(8,128)} copy(f32[1,4,512,512]{2,0,3,1:T(1,128)} %bitcast.75) | data formatting | bytes 8388608 | tf_op jit(solution)/shard_map/all_to_all | solution.py:76
  222.0 3.2 %fusion.33 = f32[2048]{0:T(1024)S(1)} fusion(bf16[1,2048,512]{2,1,0:T(8,128)(2,1)S(1)} %get-tuple-element.23, f32[1,4,512,512]{3,2,1,0:T(8,128)} %copy.11, f32[2048]{0:T(1024)S(1)} %bitcast.77), kind=kLoop, calls=%fused_computation.63 | loop fusion | flops 4192256 | bytes 6307840 | tf_op jit(solution)/shard_map/reduce_sum | solution.py:77
  225.2 8.7 %psum.29 = f32[2048]{0:T(1024)S(1)} all-reduce(f32[2048]{0:T(1024)S(1)} %broadcast_multiply_fusion.2), channel_id=1, replica_groups=mesh['seq'=8,'chan'=4] {'chan'}, use_global_device_ids=true, to_apply=%region_3.4 | all-reduce | flops 2048 | bytes 16384 | tf_op jit(solution)/shard_map/psum | solution.py:77
  233.9 0.0 copy-start
  233.9 0.0 copy-start.1
  234.0 0.0 copy-start.2
  234.0 15.5 %fusion.32 = (f32[512]{0:T(512)S(1)}, f32[512]{0:T(512)S(1)}, f32[512]{0:T(512)S(1)}, f32[512]{0:T(512)S(1)}, f32[512]{0:T(512)S(1)}, /*index=5*/f32[512]{0:T(512)S(1)}, f32[512]{0:T(512)S(1)}, f32[1,2048,512]{2,1,0:T(8,128)S(1)}) fusion(bf16[1,2048,512]{2,1,0:T(8,128)(2,1)} %param.6, f32[1,2048,512]{2,1,0:T(8,128)} %get-tuple-element.24, ...), kind=kLoop, calls=%fused_computation.62 | loop fusion | flops 28307968 | bytes 16807936 | tf_op jit(solution)/shard_map/reduce_sum | solution.py:38
  249.5 0.0 copy-done
  249.5 0.0 copy-done.1
  249.5 0.0 copy-done.2
  249.5 5.7 %fusion.19 = (f32[512]{0:T(512)S(1)}, f32[512]{0:T(512)S(1)}, f32[512]{0:T(512)S(1)}, f32[512]{0:T(512)S(1)}, f32[512]{0:T(512)S(1)}, /*index=5*/f32[512]{0:T(512)S(1)}, f32[512]{0:T(512)S(1)}, f32[1,2048,512]{2,1,0:T(8,128)S(1)}) fusion(bf16[1,2048,512]{2,1,0:T(8,128)(2,1)S(1)} %copy-done.2, f32[1,2048,512]{2,1,0:T(8,128)S(1)} %copy-done.1, ...), kind=kLoop, calls=%fused_computation.49 | loop fusion | flops 28307968 | bytes 16807936 | tf_op jit(solution)/shard_map/reduce_sum | solution.py:38
  255.2 8.1 %add_convert_fusion = (bf16[1,2048,512]{2,1,0:T(8,128)(2,1)}, bf16[1,2048,512]{2,1,0:T(8,128)(2,1)}) fusion(f32[1,2048,512]{2,1,0:T(8,128)S(1)} %get-tuple-element.20, f32[512]{0:T(512)S(1)} %bitcast.106, f32[512]{0:T(512)S(1)} %bitcast.108, f32[512]{0:T(512)S(1)} %bitcast.98, f32[512]{0:T(512)S(1)} %bitcast.100, f32[512]{0:T(512)S(1)} %bitcast.102, ...), kind=kLoop, calls=%fused_computation.70 | loop fusion | flops 29360128 | bytes 12611584 | tf_op jit(solution)/shard_map/convert_element_type | solution.py:82
  263.4 26.0 %all-reduce.4 = (f32[7,512]{1,0:T(8,128)S(1)}, f32[7,512]{1,0:T(8,128)S(1)}) all-reduce(f32[7,512]{1,0:T(8,128)S(1)} %stack.55, f32[7,512]{1,0:T(8,128)S(1)} %stack.63), channel_id=1, replica_groups=mesh['seq'=8,'chan'=4] {'seq'}, use_global_device_ids=true, to_apply=%region_11.12 | all-reduce | flops 7168 | bytes 57344 | tf_op jit(solution)/shard_map/psum | solution.py:84
  289.4 0.6 broadcast_multiply_fusion
  (4 shorter events, 0.1 us)
Async XLA Ops:
  7.2 121.0 %all-gather.2.cloned.1.call-start = ((), (), s32[]{:S(2)}) async-start(), calls=%async_computation.1 | async-start | bytes 10485760 | tf_op jit(solution)/shard_map/all_gather | solution.py:74
  233.9 15.5 %copy-start = (f32[1,4,512,512]{3,2,1,0:T(8,128)S(1)}, f32[1,4,512,512]{3,2,1,0:T(8,128)}, u32[]{:S(2)}) copy-start(f32[1,4,512,512]{3,2,1,0:T(8,128)} %copy.11) | copy-start | bytes 12582916
  233.9 15.5 %copy-start.1 = (f32[1,2048,512]{2,1,0:T(8,128)S(1)}, f32[1,2048,512]{2,1,0:T(8,128)}, u32[]{:S(2)}) copy-start(f32[1,2048,512]{2,1,0:T(8,128)} %get-tuple-element.25) | copy-start | bytes 12582916
  234.0 15.5 %copy-start.2 = (bf16[1,2048,512]{2,1,0:T(8,128)(2,1)S(1)}, bf16[1,2048,512]{2,1,0:T(8,128)(2,1)}, u32[]{:S(2)}) copy-start(bf16[1,2048,512]{2,1,0:T(8,128)(2,1)} %param.5) | copy-start | bytes 6291460
Sparse Core Ops, SparseCore 0:
  41.4 86.7 all-gather.1
where the time goes:
time: 298 us; the launch traced here: 297 us
  blocking collectives  99.9 us (34%)
  waiting for transfers between devices  86.9 us (29%)
  other arithmetic  53.6 us (18%)
  local copies, waits for them, and re-layouts  23.9 us (8%)
  matrix products  18.4 us (6%)
  between operations  14.1 us (5%)
    all_gather x1, waiting for transfers between devices, on_device(): lax.all_gather(normed_f.astype(jnp.bfloat16), 'chan', axis=2, tiled=True)  86.9 us
    all_to_all x1, blocking collectives, on_device(): lax.all_to_all(row_part, 'chan', split_axis=2, concat_axis=1, tiled=True)  53.7 us
    psum x1, blocking collectives, on_device(): lax.psum((tap_sums(gate_conv_grad, gate_raw), tap_sums(value_conv_grad, v...  26 us
    reduce_sum x2, other arithmetic, tap_sums(): jnp.sum(upstream * padded[:, TAPS - 1 - tap_index:TAPS - 1 - tap_index +...  21.2 us
    reduce_sum x1, other arithmetic, on_device(): square_total = lax.psum(jnp.sum(hidden_f * hidden_f, axis=2), 'chan')  18.7 us
    dot_general x1, matrix products, gram_rows(): jnp.einsum('srt,std->srd', residue, normed, preferred_element_type=jnp.fl...  18.4 us
    psum x1, blocking collectives, on_device(): square_total = lax.psum(jnp.sum(hidden_f * hidden_f, axis=2), 'chan')  11.5 us
    all_to_all x1, local copies, waits for them, and re-layouts, on_device(): lax.all_to_all(row_part, 'chan', split_axis=2, concat_axis=1, tiled=True)  10.9 us
  transfers between devices with their start and end apart: 1, of which 1 were waited for; matrix products, arithmetic and copies ran while one was open for 0% of the time, Pallas kernels for 0%

commit v1 on v0

v1 whole, which is shorter than its diff:
```python
import functools
import math

import jax
import jax.numpy as jnp
from jax import lax
from jax.experimental import pallas as pl
from jax.experimental.pallas import tpu as pltpu
from jax.sharding import PartitionSpec as P

epsilon = 1e-06
PAD = 16
TILE = 64
MESH = pl.DeviceIdType.MESH


def kernel(
    groups, rings, taps, norm_factor,
    gate_in, value_in, filter_gate, filter_value, teacher_in,
    gate_out, value_out, gate_taps, value_taps,
    raw_g, raw_v, conv_g, conv_v, held, teach, own_n, block_n, total, outgoing, hgrad,
    out_g, out_v, sums, mine, others,
    in_sem, out_sem, send_sem, recv_sem, fwd_sem, a2a_send, a2a_recv, tap_send, tap_recv,
):
    length, width = gate_in.shape[1:]
    stripe = length // groups
    full = width * groups
    factor = 16.0 / math.sqrt(length)
    tile = min(TILE, stripe)
    lanes = [slice(k, min(k + 128, width)) for k in range(0, width, 128)]
    f32, bf16 = jnp.float32, jnp.bfloat16
    me, ring = lax.axis_index("chan"), lax.axis_index("seq")
    square = groups == 4

    def rows_of(chunk, size=stripe, start=0):
        return pl.ds(pl.multiple_of(chunk * stripe + start, math.gcd(stripe, start) if start else stripe), size)

    in_copies = []
    for c in range(groups):
        span = pl.ds(c * stripe, stripe)
        dest = pl.ds(PAD + c * stripe, stripe)
        for k, (src, dst) in enumerate(((gate_in, raw_g), (value_in, raw_v))):
            in_copies.append(pltpu.make_async_copy(src.at[0, span], dst.at[dest], in_sem.at[k, c]))
    for copy in in_copies:
        copy.start()
    teach_copy = pltpu.make_async_copy(teacher_in.at[0], teach, in_sem.at[2, 0])
    teach_copy.start()

    barrier = pltpu.get_barrier_semaphore()
    for step in range(1, groups):
        pl.semaphore_signal(barrier, inc=1, device_id=(ring, lax.rem(me + step, groups)), device_id_type=MESH)
    for step in range(1, rings):
        pl.semaphore_signal(barrier, inc=1, device_id=(lax.rem(ring + step, rings), me), device_id_type=MESH)

    raw_g[0:PAD] = jnp.zeros((PAD, width), bf16)
    raw_v[0:PAD] = jnp.zeros((PAD, width), bf16)
    conv_g[length:] = jnp.zeros((PAD, width), f32)
    conv_v[length:] = jnp.zeros((PAD, width), f32)
    hgrad[length:] = jnp.zeros((PAD, width), bf16)
    sums[...] = jnp.zeros(sums.shape, f32)
    total[...] = jnp.zeros(total.shape, f32)
    for copy in in_copies:
        copy.wait()

    def conv_chunk(chunk):
        def body(i, _):
            base = pl.multiple_of(chunk * stripe + i * tile, tile)
            for lane in lanes:
                made = []
                for raw, weights, store in ((raw_g, filter_gate, conv_g), (raw_v, filter_value, conv_v)):
                    window = raw[pl.ds(base, tile + PAD), lane].astype(f32)
                    out = weights[0:1, lane] * window[PAD:]
                    for j in range(1, taps):
                        out = out + weights[j : j + 1, lane] * pltpu.roll(window, j, 0)[PAD:]
                    store[pl.ds(base, tile), lane] = out
                    made.append(out)
                held[me, pl.ds(base, tile), lane] = (made[0] * made[1]).astype(bf16)
            return 0

        lax.fori_loop(0, stripe // tile, body, 0)

    def gather_copy(source, rows, device, send, recv):
        block = held.at[source, rows]
        return pltpu.make_async_remote_copy(
            src_ref=block, dst_ref=block, send_sem=send, recv_sem=recv,
            device_id=(ring, device), device_id_type=MESH,
        )

    started = []
    if square:
        across = me + 1 - 2 * lax.rem(me, 2)
        along = lax.rem(me + 2, 4)
        corner = 3 - me

        def send(to, k, chunk):
            copy = gather_copy(me, rows_of(chunk), to, send_sem.at[k, chunk], recv_sem.at[me, chunk])
            copy.start()
            started.append(copy)

        conv_chunk(across)
        pl.semaphore_wait(barrier, groups + rings - 2)
        send(across, 0, across)
        conv_chunk(along)
        send(along, 1, along)
        conv_chunk(corner)
        send(across, 0, corner)
        send(along, 1, corner)
        send(across, 0, along)
        send(along, 1, across)
        conv_chunk(me)
        send(across, 0, me)
        send(along, 1, me)
        half = stripe // 2
        for from_x, from_y in ((me, me), (along, across), (corner, corner), (across, along)):
            for k, (source, chunk, to, start, slot) in enumerate(
                ((across, from_x, along, 0, 0), (along, from_y, across, half, 1))
            ):
                gather_copy(source, rows_of(chunk), me, send_sem.at[0, 0], recv_sem.at[source, chunk]).wait_recv()
                signal = recv_sem.at[source if slot == 0 else to, chunk]
                copy = gather_copy(source, rows_of(chunk, half, start), to, fwd_sem.at[k, chunk], signal)
                copy.start()
                started.append(copy)
    else:
        for c in range(groups):
            conv_chunk(c)
        pl.semaphore_wait(barrier, groups + rings - 2)

        def send_all(copy_do):
            def body(i, _):
                chunk, step = i // (groups - 1), 1 + lax.rem(i, groups - 1)
                copy_do(
                    gather_copy(
                        me, rows_of(chunk), lax.rem(me + step, groups),
                        send_sem.at[step, chunk], recv_sem.at[me, chunk],
                    )
                )
                return 0

            lax.fori_loop(0, groups * (groups - 1), body, 0)

        send_all(lambda copy: copy.start())

    def wait_chunk(chunk):
        if square:
            gather_copy(corner, rows_of(chunk, half), me, send_sem.at[0, 0], recv_sem.at[corner, chunk]).wait_recv()
            gather_copy(corner, rows_of(chunk, half, half), me, send_sem.at[0, 0], recv_sem.at[me, chunk]).wait_recv()
        else:
            def body(step, _):
                source = lax.rem(me + step, groups)
                gather_copy(source, rows_of(chunk), me, send_sem.at[0, 0], recv_sem.at[source, chunk]).wait_recv()
                return 0

            lax.fori_loop(1, groups, body, 0)

    norm_tile = min(32, stripe)

    def scale_of(base):
        squares = jnp.zeros((norm_tile, width), f32)
        for g in range(groups):
            block = held[g, pl.ds(base, norm_tile)].astype(f32)
            squares = squares + block * block
        return lax.rsqrt(jnp.sum(squares, axis=1, keepdims=True) / full + epsilon)

    def normalize(chunk, dest):
        def body(i, _):
            base = pl.multiple_of(chunk * stripe + i * norm_tile, norm_tile)
            inverse = scale_of(base)
            for g in range(groups):
                block = held[g, pl.ds(base, norm_tile)].astype(f32)
                dest[pl.ds(pl.multiple_of(i * norm_tile, norm_tile), norm_tile), g * width : (g + 1) * width] = (
                    block * inverse
                ).astype(bf16)
            return 0

        lax.fori_loop(0, stripe // norm_tile, body, 0)

    teach_copy.wait()
    mat = min(256, stripe)

    def gram_chunk(t, _):
        chunk = lax.rem(me + t, groups)
        wait_chunk(chunk)
        normalize(chunk, block_n)

        @pl.when(t == 0)
        def _():
            own_n[...] = block_n[...]

        def body(m, _):
            rows = pl.ds(pl.multiple_of(m * mat, mat), mat)
            similarity = lax.dot_general(
                own_n[rows], block_n[...], (((1,), (1,)), ((), ())), preferred_element_type=f32
            ) / full
            residue = (factor * (similarity - teach[rows, rows_of(chunk)])).astype(bf16)
            total[rows] += jnp.dot(residue, block_n[...], preferred_element_type=f32)
            return 0

        lax.fori_loop(0, stripe // mat, body, 0)
        return 0

    lax.fori_loop(0, groups, gram_chunk, 0)

    def finish(i, _):
        local = pl.multiple_of(i * norm_tile, norm_tile)
        base = pl.multiple_of(me * stripe + i * norm_tile, norm_tile)
        rows = pl.ds(local, norm_tile)
        inverse = scale_of(base)
        inner = jnp.zeros((norm_tile, width), f32)
        for g in range(groups):
            part = slice(g * width, (g + 1) * width)
            inner = inner + held[g, pl.ds(base, norm_tile)].astype(f32) * inverse * total[rows, part]
        projection = jnp.sum(inner, axis=1, keepdims=True) / full
        for g in range(groups):
            part = slice(g * width, (g + 1) * width)
            normed = held[g, pl.ds(base, norm_tile)].astype(f32) * inverse
            outgoing[g, rows] = (inverse * (total[rows, part] - normed * projection)).astype(bf16)
        return 0

    pieces = 2
    piece = stripe // pieces
    steps = piece // norm_tile

    def exchange(target, p, source_row):
        return pltpu.make_async_remote_copy(
            src_ref=outgoing.at[target, pl.ds(p * piece, piece)],
            dst_ref=hgrad.at[rows_of(source_row, piece, p * piece)],
            send_sem=a2a_send.at[target, p], recv_sem=a2a_recv.at[source_row, p],
            device_id=(ring, target), device_id_type=MESH,
        )

    for p in range(pieces):
        lax.fori_loop(p * steps, (p + 1) * steps, finish, 0)
        for step in range(1, groups):
            exchange(lax.rem(me + groups - step, groups), p, me).start()
    hgrad[rows_of(me)] = outgoing[me]

    def back_tile(base):
        for k in range(0, width, 128):
            lane = slice(k, min(k + 128, width))
            up = hgrad[pl.ds(base, tile + PAD), lane].astype(f32)
            for b, (conv, raw, weights, store) in enumerate(
                ((conv_v, raw_g, filter_gate, out_g), (conv_g, raw_v, filter_value, out_v))
            ):
                window = up * conv[pl.ds(base, tile + PAD), lane]
                signal = raw[pl.ds(pl.multiple_of(base + PAD, PAD), tile), lane].astype(f32)
                out = None
                for j in range(taps):
                    shifted = (window if j == 0 else pltpu.roll(window, tile + PAD - j, 0))[:tile]
                    term = weights[j : j + 1, lane] * shifted
                    out = term if out is None else out + term
                    product = shifted * signal
                    folded = product[0:8]
                    for r in range(8, tile, 8):
                        folded = folded + product[r : r + 8]
                    sums[b, j, :, lane] += folded
                store[pl.ds(base, tile), lane] = out.astype(bf16)

    tiles = stripe // tile
    for step in range(groups):
        source = lax.rem(me + step, groups)
        if step:
            for p in range(pieces):
                exchange_in = pltpu.make_async_remote_copy(
                    src_ref=outgoing.at[source, pl.ds(p * piece, piece)],
                    dst_ref=hgrad.at[rows_of(source, piece, p * piece)],
                    send_sem=a2a_send.at[source, p], recv_sem=a2a_recv.at[source, p],
                    device_id=(ring, source), device_id_type=MESH,
                )
                exchange_in.wait_recv()

        def inner_tiles(i, _, source=source):
            back_tile(pl.multiple_of(source * stripe + i * tile, tile))
            return 0

        lax.fori_loop(0, tiles - 1, inner_tiles, 0)

    def last_tiles(c, _):
        back_tile(pl.multiple_of(c * stripe + (tiles - 1) * tile, tile))
        return 0

    lax.fori_loop(0, groups, last_tiles, 0)
    out_copies = [
        pltpu.make_async_copy(src, dst.at[0], out_sem.at[k])
        for k, (src, dst) in enumerate(((out_g, gate_out), (out_v, value_out)))
    ]
    for copy in out_copies:
        copy.start()

    for b in range(2):
        for j in range(taps):
            mine[b, j : j + 1] = jnp.sum(sums[b, j], axis=0, keepdims=True)
        mine[b, taps:] = jnp.zeros((8 - taps, width), f32)

    def tap_copy(to, slot):
        return pltpu.make_async_remote_copy(
            src_ref=mine, dst_ref=others.at[slot], send_sem=tap_send.at[slot], recv_sem=tap_recv.at[slot],
            device_id=(to, me), device_id_type=MESH,
        )

    tap_copies = [tap_copy(lax.rem(ring + step, rings), step) for step in range(1, rings)]
    for copy in tap_copies:
        copy.start()
    summed = [mine[b] for b in range(2)]
    for step, copy in enumerate(tap_copies):
        copy.wait_recv()
        summed = [summed[b] + others[step + 1, b] for b in range(2)]
    gate_taps[...] = summed[0][:taps] * norm_factor
    value_taps[...] = summed[1][:taps] * norm_factor

    for copy in tap_copies:
        copy.wait_send()
    if square:
        for copy in started:
            copy.wait_send()
    else:
        send_all(lambda copy: copy.wait_send())
    for step in range(1, groups):
        for p in range(pieces):
            exchange(lax.rem(me + groups - step, groups), p, me).wait_send()
    for copy in out_copies:
        copy.wait()


def on_device(gate_raw, value_raw, filter_gate, filter_value, teacher):
    seq_count, length, width = gate_raw.shape
    groups, rings = lax.axis_size("chan"), lax.axis_size("seq")
    taps = filter_gate.shape[0]
    stripe, full = length // groups, width * groups
    norm_factor = 1.0 / math.sqrt(rings * seq_count * length)
    f32, bf16 = jnp.float32, jnp.bfloat16
    any_space = pl.BlockSpec(memory_space=pl.ANY)
    vmem = pl.BlockSpec(memory_space=pltpu.VMEM)
    dma = pltpu.SemaphoreType.DMA
    return pl.pallas_call(
        functools.partial(kernel, groups, rings, taps, norm_factor),
        out_shape=(
            jax.ShapeDtypeStruct(gate_raw.shape, bf16),
            jax.ShapeDtypeStruct(gate_raw.shape, bf16),
            jax.ShapeDtypeStruct((taps, width), f32),
            jax.ShapeDtypeStruct((taps, width), f32),
        ),
        in_specs=[any_space, any_space, vmem, vmem, any_space],
        out_specs=(any_space, any_space, vmem, vmem),
        scratch_shapes=[
            pltpu.VMEM((length + PAD, width), bf16),
            pltpu.VMEM((length + PAD, width), bf16),
            pltpu.VMEM((length + PAD, width), f32),
            pltpu.VMEM((length + PAD, width), f32),
            pltpu.VMEM((groups, length, width), bf16),
            pltpu.VMEM((stripe, length), f32),
            pltpu.VMEM((stripe, full), bf16),
            pltpu.VMEM((stripe, full), bf16),
            pltpu.VMEM((stripe, full), f32),
            pltpu.VMEM((groups, stripe, width), bf16),
            pltpu.VMEM((length + PAD, width), bf16),
            pltpu.VMEM((length, width), bf16),
            pltpu.VMEM((length, width), bf16),
            pltpu.VMEM((2, taps, 8, width), f32),
            pltpu.VMEM((2, 8, width), f32),
            pltpu.VMEM((rings, 2, 8, width), f32),
            dma((3, groups)),
            dma((2,)),
            dma((groups, groups)),
            dma((groups, groups)),
            dma((2, groups)),
            dma((groups, 2)),
            dma((groups, 2)),
            dma((rings,)),
            dma((rings,)),
        ],
        compiler_params=pltpu.CompilerParams(
            collective_id=0, has_side_effects=True, vmem_limit_bytes=60 * 1024 * 1024
        ),
    )(gate_raw, value_raw, filter_gate, filter_value, teacher)


def solution(mesh):
    placed = (
        P("seq", None, "chan"),
        P("seq", None, "chan"),
        P(None, "chan"),
        P(None, "chan"),
        P("seq", "chan", None),
    )
    return jax.shard_map(
        on_device,
        mesh=mesh,
        in_specs=placed,
        out_specs=(
            P("seq", None, "chan"),
            P("seq", None, "chan"),
            P(None, "chan"),
            P(None, "chan"),
        ),
        check_vma=False,
    )
```

time: 298 us -> 137 us (0.46)
  Pallas kernels: 0 us -> 130 us
  blocking collectives: 99.9 us -> 0 us
  waiting for transfers between devices: 86.9 us -> 0 us
  other arithmetic: 53.6 us -> 0 us
  matrix products: 18.4 us -> 0 us
  local copies, waits for them, and re-layouts: 23.9 us -> 5.73 us
  between operations: 14.1 us -> 0.65 us
    pallas_call x0 -> x1, Pallas kernels: none -> 130 us  [on_device(): pl.pallas_call(functools.partial(kernel, groups, rings, taps, norm_factor...]
    all_gather x1 -> x0, waiting for transfers between devices: 86.9 us -> none  [on_device(): lax.all_gather(normed_f.astype(jnp.bfloat16), 'chan', axis=2, tiled=True)]
    all_to_all x1 -> x0, blocking collectives: 53.7 us -> none  [on_device(): lax.all_to_all(row_part, 'chan', split_axis=2, concat_axis=1, tiled=True)]
    psum x3 -> x0, blocking collectives: 46.3 us -> none  [the longest x1 26 us: on_device(): lax.psum((tap_sums(gate_conv_grad, gate_raw), tap_sums(value_conv_grad, v...]
    reduce_sum x4 -> x0, other arithmetic: 43 us -> none  [the longest x2 21.2 us: tap_sums(): jnp.sum(upstream * padded[:, TAPS - 1 - tap_index:TAPS - 1 - tap_index +...]
    dot_general x1 -> x0, matrix products: 18.4 us -> none  [gram_rows(): jnp.einsum('srt,std->srd', residue, normed, preferred_element_type=jnp.fl...]
    all_to_all x1 -> x0, local copies, waits for them, and re-layouts: 10.9 us -> none  [on_device(): lax.all_to_all(row_part, 'chan', split_axis=2, concat_axis=1, tiled=True)]
    dot_general x1 -> x0, local copies, waits for them, and re-layouts: 10.9 us -> none  [gram_rows(): jnp.einsum('srt,std->srd', residue, normed, preferred_element_type=jnp.fl...]
  transfers between devices with their start and end apart: 1 -> 0, of which waited for: 1 -> 0; matrix products, arithmetic and copies ran while one was open for 0% -> 0% of each run, Pallas kernels for 0% -> 0%
where the time goes in v1:
time: 137 us; the launch traced here: 136 us
  Pallas kernels  130 us (95%)
  local copies, waits for them, and re-layouts  5.73 us (4%)
    pallas_call x1, Pallas kernels, on_device(): pl.pallas_call(functools.partial(kernel, groups, rings, taps, norm_factor...  130 us
    unnamed x10, local copies, waits for them, and re-layouts  5.73 us

profile of v1, /device:TPU:0, one launch (start us, length us, event | category | flops | bytes accessed | tf_op | source)
XLA Modules:
  0.0 136.3 jit_solution(10252907641331954241)
XLA Ops:
  0.6 129.9 %shard_map.84 = (bf16[1,2048,512]{2,1,0:T(8,128)(2,1)}, bf16[1,2048,512]{2,1,0:T(8,128)(2,1)}, f32[7,512]{1,0:T(8,128)}, f32[7,512]{1,0:T(8,128)}) custom-call(bf16[1,2048,512]{2,1,0:T(8,128)(2,1)} %gate_in.1, bf16[1,2048,512]{2,1,0:T(8,128)(2,1)} %value_in.1, f32[7,512]{1,0:T(8,128)} %filter_gate.1, f32[7,512]{1,0:T(8,128)} %filter_value.1, ...), custom_call_target="tpu_custom_call" | custom-call | tf_op jit(solution)/shard_map/pallas_call | solution.py:334
  130.6 0.0 copy-start
  130.6 3.2 %copy.13 = bf16[1,2048,512]{2,1,0:T(8,128)(2,1)} copy(bf16[1,2048,512]{2,1,0:T(8,128)(2,1)} %get-tuple-element.8) | data formatting | bytes 4194304
  133.8 0.0 copy-done
  133.8 0.0 copy-start.2
  133.8 0.0 copy-start.1
  133.8 1.3 copy.14
  135.1 0.0 copy-done.2
  135.1 0.6 copy.15
  135.7 0.0 copy-done.1
  135.7 0.6 copy.16
Async XLA Ops:
  130.6 3.2 %copy-start = (bf16[1,2048,512]{2,1,0:T(8,128)(2,1)S(1)}, bf16[1,2048,512]{2,1,0:T(8,128)(2,1)}, u32[]{:S(2)}) copy-start(bf16[1,2048,512]{2,1,0:T(8,128)(2,1)} %get-tuple-element.9) | copy-start | bytes 6291460
  133.8 1.3 copy-start.2
  133.8 1.9 %copy-start.1 = (f32[7,512]{1,0:T(8,128)S(1)}, f32[7,512]{1,0:T(8,128)}, u32[]{:S(2)}) copy-start(f32[7,512]{1,0:T(8,128)} %get-tuple-element.11) | copy-start | bytes 43012

commit v2 on v1

--- a/solution.py
+++ b/solution.py
@@ -20,7 +20,8 @@
     gate_out, value_out, gate_taps, value_taps,
     raw_g, raw_v, conv_g, conv_v, held, teach, own_n, block_n, total, outgoing, hgrad,
     out_g, out_v, sums, mine, others,
-    in_sem, out_sem, send_sem, recv_sem, fwd_sem, a2a_send, a2a_recv, tap_send, tap_recv,
+    in_sem, out_sem, send_sem, recv_sem, a2a_send, a2a_recv, tap_send, tap_recv,
+    near, teach_send_sem, teach_recv_sem,
 ):
     length, width = gate_in.shape[1:]
     stripe = length // groups
@@ -30,7 +31,21 @@
     lanes = [slice(k, min(k + 128, width)) for k in range(0, width, 128)]
     f32, bf16 = jnp.float32, jnp.bfloat16
     me, ring = lax.axis_index("chan"), lax.axis_index("seq")
-    square = groups == 4
+    paired = groups == 4 and rings % 2 == 0
+    flip1 = lambda at: at + 1 - 2 * lax.rem(at, 2)
+    flip2 = lambda at: lax.rem(at + 2, 4)
+    flip3 = lambda at: 3 - at
+    if paired:
+        core = lax.rem(ring, 2)
+        buddy = ring + 1 - 2 * core
+        side = me // 2
+        same = 1 - (core - side) * (core - side)
+        base_at = same * me + (1 - same) * flip2(me)
+        slot = same * me + (1 - same) * groups
+        proc = ring - core + side
+        is_home, is_guest = same == 1, same == 0
+    else:
+        base_at, slot, proc = me, me, ring
 
     def rows_of(chunk, size=stripe, start=0):
         return pl.ds(pl.multiple_of(chunk * stripe + start, math.gcd(stripe, start) if start else stripe), size)
@@ -44,11 +59,17 @@
     for copy in in_copies:
         copy.start()
     teach_copy = pltpu.make_async_copy(teacher_in.at[0], teach, in_sem.at[2, 0])
-    teach_copy.start()
+    if paired:
+        pl.when(is_home)(teach_copy.start)
+    else:
+        teach_copy.start()
 
     barrier = pltpu.get_barrier_semaphore()
     for step in range(1, groups):
         pl.semaphore_signal(barrier, inc=1, device_id=(ring, lax.rem(me + step, groups)), device_id_type=MESH)
+        if paired:
+            pl.semaphore_signal(barrier, inc=1, device_id=(buddy, lax.rem(me + step, groups)), device_id_type=MESH)
+    greeted = (groups - 1) * (2 if paired else 1) + rings - 1
     for step in range(1, rings):
         pl.semaphore_signal(barrier, inc=1, device_id=(lax.rem(ring + step, rings), me), device_id_type=MESH)
 
@@ -74,80 +95,118 @@
                         out = out + weights[j : j + 1, lane] * pltpu.roll(window, j, 0)[PAD:]
                     store[pl.ds(base, tile), lane] = out
                     made.append(out)
-                held[me, pl.ds(base, tile), lane] = (made[0] * made[1]).astype(bf16)
+                held[slot, pl.ds(base, tile), lane] = (made[0] * made[1]).astype(bf16)
             return 0
 
         lax.fori_loop(0, stripe // tile, body, 0)
 
-    def gather_copy(source, rows, device, send, recv):
-        block = held.at[source, rows]
+    def gather_copy(source, target, chunk, to, send):
+        rows = rows_of(chunk)
         return pltpu.make_async_remote_copy(
-            src_ref=block, dst_ref=block, send_sem=send, recv_sem=recv,
-            device_id=(ring, device), device_id_type=MESH,
+            src_ref=held.at[source, rows], dst_ref=held.at[target, rows],
+            send_sem=send, recv_sem=recv_sem.at[target, chunk],
+            device_id=to, device_id_type=MESH,
         )
 
-    started = []
-    if square:
-        across = me + 1 - 2 * lax.rem(me, 2)
-        along = lax.rem(me + 2, 4)
-        corner = 3 - me
-
-        def send(to, k, chunk):
-            copy = gather_copy(me, rows_of(chunk), to, send_sem.at[k, chunk], recv_sem.at[me, chunk])
-            copy.start()
-            started.append(copy)
-
-        conv_chunk(across)
-        pl.semaphore_wait(barrier, groups + rings - 2)
-        send(across, 0, across)
-        conv_chunk(along)
-        send(along, 1, along)
-        conv_chunk(corner)
-        send(across, 0, corner)
-        send(along, 1, corner)
-        send(across, 0, along)
-        send(along, 1, across)
-        conv_chunk(me)
-        send(across, 0, me)
-        send(along, 1, me)
-        half = stripe // 2
-        for from_x, from_y in ((me, me), (along, across), (corner, corner), (across, along)):
-            for k, (source, chunk, to, start, slot) in enumerate(
-                ((across, from_x, along, 0, 0), (along, from_y, across, half, 1))
-            ):
-                gather_copy(source, rows_of(chunk), me, send_sem.at[0, 0], recv_sem.at[source, chunk]).wait_recv()
-                signal = recv_sem.at[source if slot == 0 else to, chunk]
-                copy = gather_copy(source, rows_of(chunk, half, start), to, fwd_sem.at[k, chunk], signal)
-                copy.start()
-                started.append(copy)
+    def arrived(source, chunk):
+        gather_copy(source, source, chunk, (ring, me), send_sem.at[0, 0]).wait_recv()
+
+    if paired:
+        far = pl.ds(pl.multiple_of(side * 2 * stripe, stripe), 2 * stripe)
+
+        def teach_send(cols, dst, to, k):
+            return pltpu.make_async_remote_copy(
+                src_ref=teacher_in.at[0, :, cols], dst_ref=dst, send_sem=teach_send_sem.at[k],
+                recv_sem=teach_recv_sem.at[k], device_id=to, device_id_type=MESH,
+            )
+
+        to_swap = teach_send(far, teach.at[:, far], (buddy, flip2(me)), 0)
+        to_near = teach_send(rows_of(flip2(me)), near.at[0], (buddy, me), 1)
+        to_next = teach_send(rows_of(flip3(me)), near.at[1], (buddy, flip1(me)), 2)
+        far_in = pl.ds(pl.multiple_of((1 - side) * 2 * stripe, stripe), 2 * stripe)
+
+        def to_x(chunk):
+            return gather_copy(base_at, base_at, chunk, (ring, flip1(me)), send_sem.at[0, chunk])
+
+        def to_buddy(chunk):
+            return gather_copy(base_at, base_at, chunk, (buddy, me), send_sem.at[1, chunk])
+
+        def pass_on(chunk):
+            return gather_copy(flip1(base_at), flip1(base_at), chunk, (buddy, me), send_sem.at[2, chunk])
+
+        def swap(chunk):
+            return gather_copy(groups, me, chunk, (buddy, flip2(me)), send_sem.at[3, chunk])
+
+        order = (flip1(me), flip3(me), me, flip2(me))
+        pl.semaphore_wait(barrier, greeted)
+
+        @pl.when(is_home)
+        def _():
+            to_near.start()
+            to_next.start()
+
+        for chunk in order:
+            conv_chunk(chunk)
+
+            @pl.when(is_home)
+            def _(chunk=chunk):
+                to_x(chunk).start()
+                to_buddy(chunk).start()
+
+            @pl.when(is_guest)
+            def _(chunk=chunk):
+                swap(chunk).start()
+
+        @pl.when(is_guest)
+        def _():
+            to_swap.start()
+            for chunk in (flip3(me), flip1(me), flip2(me), me):
+                arrived(base_at, chunk)
+                to_x(chunk).start()
+                to_buddy(chunk).start()
+            for k in range(2):
+                teach_send(rows_of(0), near.at[k], (ring, me), 1 + k).wait_recv()
+                at = me if k == 0 else flip1(me)
+
+                def turn(i, _, k=k, at=at):
+                    rows = pl.ds(pl.multiple_of(i * 128, 128), 128)
+                    for c in range(0, stripe, 128):
+                        cols = pl.ds(pl.multiple_of(at * stripe + c, 128), 128)
+                        teach[rows, cols] = near[k, c : c + 128, rows].T
+                    return 0
+
+                lax.fori_loop(0, stripe // 128, turn, 0)
+
+        for chunk in (base_at, flip2(base_at)):
+            arrived(flip1(base_at), chunk)
+            pass_on(chunk).start()
     else:
         for c in range(groups):
             conv_chunk(c)
-        pl.semaphore_wait(barrier, groups + rings - 2)
+        pl.semaphore_wait(barrier, greeted)
 
         def send_all(copy_do):
             def body(i, _):
                 chunk, step = i // (groups - 1), 1 + lax.rem(i, groups - 1)
-                copy_do(
-                    gather_copy(
-                        me, rows_of(chunk), lax.rem(me + step, groups),
-                        send_sem.at[step, chunk], recv_sem.at[me, chunk],
-                    )
-                )
+                copy_do(gather_copy(me, me, chunk, (ring, lax.rem(me + step, groups)), send_sem.at[step, chunk]))
                 return 0
 
             lax.fori_loop(0, groups * (groups - 1), body, 0)
 
         send_all(lambda copy: copy.start())
 
-    def wait_chunk(chunk):
-        if square:
-            gather_copy(corner, rows_of(chunk, half), me, send_sem.at[0, 0], recv_sem.at[corner, chunk]).wait_recv()
-            gather_copy(corner, rows_of(chunk, half, half), me, send_sem.at[0, 0], recv_sem.at[me, chunk]).wait_recv()
+    def wait_chunk(t, chunk):
+        if paired:
+            @pl.when(t >= 2)
+            def _():
+                arrived(flip1(base_at), chunk)
+                pass_on(chunk).start()
+
+            arrived(flip2(base_at), chunk)
+            arrived(flip3(base_at), chunk)
         else:
             def body(step, _):
-                source = lax.rem(me + step, groups)
-                gather_copy(source, rows_of(chunk), me, send_sem.at[0, 0], recv_sem.at[source, chunk]).wait_recv()
+                arrived(lax.rem(me + step, groups), chunk)
                 return 0
 
             lax.fori_loop(1, groups, body, 0)
@@ -174,12 +233,23 @@
 
         lax.fori_loop(0, stripe // norm_tile, body, 0)
 
-    teach_copy.wait()
+    if paired:
+        pl.when(is_home)(teach_copy.wait)
+
+        @pl.when(is_guest)
+        def _():
+            teach_send(far_in, teach.at[:, far_in], (ring, me), 0).wait_recv()
+    else:
+        teach_copy.wait()
     mat = min(256, stripe)
 
     def gram_chunk(t, _):
-        chunk = lax.rem(me + t, groups)
-        wait_chunk(chunk)
+        if paired:
+            late = jnp.where(t == 2, flip3(me), flip1(me))
+            chunk = jnp.where(t == 0, base_at, jnp.where(t == 1, flip2(base_at), late))
+        else:
+            chunk = lax.rem(me + t, groups)
+        wait_chunk(t, chunk)
         normalize(chunk, block_n)
 
         @pl.when(t == 0)
@@ -202,7 +272,7 @@
 
     def finish(i, _):
         local = pl.multiple_of(i * norm_tile, norm_tile)
-        base = pl.multiple_of(me * stripe + i * norm_tile, norm_tile)
+        base = pl.multiple_of(base_at * stripe + i * norm_tile, norm_tile)
         rows = pl.ds(local, norm_tile)
         inverse = scale_of(base)
         inner = jnp.zeros((norm_tile, width), f32)
@@ -216,7 +286,7 @@
             outgoing[g, rows] = (inverse * (total[rows, part] - normed * projection)).astype(bf16)
         return 0
 
-    pieces = 2
+    pieces = max(1, min(4, stripe // 128))
     piece = stripe // pieces
     steps = piece // norm_tile
 
@@ -225,14 +295,31 @@
             src_ref=outgoing.at[target, pl.ds(p * piece, piece)],
             dst_ref=hgrad.at[rows_of(source_row, piece, p * piece)],
             send_sem=a2a_send.at[target, p], recv_sem=a2a_recv.at[source_row, p],
-            device_id=(ring, target), device_id_type=MESH,
+            device_id=(proc, target), device_id_type=MESH,
         )
 
-    for p in range(pieces):
+    if paired:
+        targets = (flip3(me), flip1(me), flip2(me))
+    else:
+        targets = tuple(lax.rem(me + groups - step, groups) for step in range(1, groups))
+
+    def stay(p):
+        hgrad[rows_of(base_at, piece, p * piece)] = outgoing[me, pl.ds(p * piece, piece)]
+
+    for p in reversed(range(pieces)):
         lax.fori_loop(p * steps, (p + 1) * steps, finish, 0)
-        for step in range(1, groups):
-            exchange(lax.rem(me + groups - step, groups), p, me).start()
-    hgrad[rows_of(me)] = outgoing[me]
+        for target in targets:
+            exchange(target, p, base_at).start()
+        if paired:
+            @pl.when(is_guest)
+            def _(p=p):
+                exchange(me, p, base_at).start()
+
+            @pl.when(is_home)
+            def _(p=p):
+                stay(p)
+        else:
+            stay(p)
 
     def back_tile(base):
         for k in range(0, width, 128):
@@ -256,23 +343,26 @@
                 store[pl.ds(base, tile), lane] = out.astype(bf16)
 
     tiles = stripe // tile
-    for step in range(groups):
-        source = lax.rem(me + step, groups)
-        if step:
-            for p in range(pieces):
-                exchange_in = pltpu.make_async_remote_copy(
-                    src_ref=outgoing.at[source, pl.ds(p * piece, piece)],
-                    dst_ref=hgrad.at[rows_of(source, piece, p * piece)],
-                    send_sem=a2a_send.at[source, p], recv_sem=a2a_recv.at[source, p],
-                    device_id=(ring, source), device_id_type=MESH,
-                )
-                exchange_in.wait_recv()
-
-        def inner_tiles(i, _, source=source):
-            back_tile(pl.multiple_of(source * stripe + i * tile, tile))
-            return 0
-
-        lax.fori_loop(0, tiles - 1, inner_tiles, 0)
+    per = tiles // pieces
+    if paired:
+        sources = (base_at, flip2(base_at), flip1(base_at), flip3(base_at))
+    else:
+        sources = tuple(lax.rem(me + step, groups) for step in range(groups))
+    for p in reversed(range(pieces)):
+        for step, source in enumerate(sources):
+            def landed(p=p, source=source):
+                exchange(source, p, source).wait_recv()
+
+            if step:
+                landed()
+            elif paired:
+                pl.when(is_guest)(landed)
+
+            def inner_tiles(i, _, source=source):
+                back_tile(pl.multiple_of(source * stripe + i * tile, tile))
+                return 0
+
+            lax.fori_loop(p * per, (p + 1) * per - (1 if p == pieces - 1 else 0), inner_tiles, 0)
 
     def last_tiles(c, _):
         back_tile(pl.multiple_of(c * stripe + (tiles - 1) * tile, tile))
@@ -309,14 +399,29 @@
 
     for copy in tap_copies:
         copy.wait_send()
-    if square:
-        for copy in started:
-            copy.wait_send()
+    if paired:
+        for chunk in range(groups):
+            to_x(chunk).wait_send()
+            to_buddy(chunk).wait_send()
+            pass_on(chunk).wait_send()
+
+        @pl.when(is_home)
+        def _():
+            to_near.wait_send()
+            to_next.wait_send()
+
+        @pl.when(is_guest)
+        def _():
+            to_swap.wait_send()
+            for chunk in range(groups):
+                swap(chunk).wait_send()
+            for p in range(pieces):
+                exchange(me, p, base_at).wait_send()
     else:
         send_all(lambda copy: copy.wait_send())
-    for step in range(1, groups):
+    for target in targets:
         for p in range(pieces):
-            exchange(lax.rem(me + groups - step, groups), p, me).wait_send()
+            exchange(target, p, base_at).wait_send()
     for copy in out_copies:
         copy.wait()
 
@@ -346,7 +451,7 @@
             pltpu.VMEM((length + PAD, width), bf16),
             pltpu.VMEM((length + PAD, width), f32),
             pltpu.VMEM((length + PAD, width), f32),
-            pltpu.VMEM((groups, length, width), bf16),
+            pltpu.VMEM((groups + 1, length, width), bf16),
             pltpu.VMEM((stripe, length), f32),
             pltpu.VMEM((stripe, full), bf16),
             pltpu.VMEM((stripe, full), bf16),
@@ -362,11 +467,13 @@
             dma((2,)),
             dma((groups, groups)),
             dma((groups, groups)),
-            dma((2, groups)),
-            dma((groups, 2)),
-            dma((groups, 2)),
+            dma((groups, 4)),
+            dma((groups, 4)),
             dma((rings,)),
             dma((rings,)),
+            pltpu.VMEM((2, stripe, stripe), f32),
+            dma((3,)),
+            dma((3,)),
         ],
         compiler_params=pltpu.CompilerParams(
             collective_id=0, has_side_effects=True, vmem_limit_bytes=60 * 1024 * 1024

time: 137 us -> 121 us (0.88)
  Pallas kernels: 130 us -> 113 us
    pallas_call x1, Pallas kernels: 130 us -> 113 us  [on_device(): pl.pallas_call(functools.partial(kernel, groups, rings, taps, norm_factor...]
where the time goes in v2:
time: 121 us; the launch traced here: 120 us
  Pallas kernels  113 us (93%)
  local copies, waits for them, and re-layouts  5.73 us (5%)
    pallas_call x1, Pallas kernels, on_device(): pl.pallas_call(functools.partial(kernel, groups, rings, taps, norm_factor...  113 us
    unnamed x10, local copies, waits for them, and re-layouts  5.73 us

profile of v2, /device:TPU:0, one launch (start us, length us, event | category | flops | bytes accessed | tf_op | source)
XLA Modules:
  0.0 119.6 jit_solution(3395457495594383490)
XLA Ops:
  0.6 113.3 %shard_map.84 = (bf16[1,2048,512]{2,1,0:T(8,128)(2,1)}, bf16[1,2048,512]{2,1,0:T(8,128)(2,1)}, f32[7,512]{1,0:T(8,128)}, f32[7,512]{1,0:T(8,128)}) custom-call(bf16[1,2048,512]{2,1,0:T(8,128)(2,1)} %gate_in.1, bf16[1,2048,512]{2,1,0:T(8,128)(2,1)} %value_in.1, f32[7,512]{1,0:T(8,128)} %filter_gate.1, f32[7,512]{1,0:T(8,128)} %filter_value.1, ...), custom_call_target="tpu_custom_call" | custom-call | tf_op jit(solution)/shard_map/pallas_call | solution.py:439
  113.9 0.0 copy-start
  113.9 3.2 %copy.13 = bf16[1,2048,512]{2,1,0:T(8,128)(2,1)} copy(bf16[1,2048,512]{2,1,0:T(8,128)(2,1)} %get-tuple-element.8) | data formatting | bytes 4194304
  117.1 0.0 copy-done
  117.1 0.0 copy-start.2
  117.1 0.0 copy-start.1
  117.1 1.3 %copy.14 = bf16[1,2048,512]{2,1,0:T(8,128)(2,1)} copy(bf16[1,2048,512]{2,1,0:T(8,128)(2,1)S(1)} %copy-done) | data formatting | bytes 4194304
  118.4 0.0 copy-done.2
  118.4 0.6 copy.15
  119.0 0.0 copy-done.1
  119.0 0.6 copy.16
Async XLA Ops:
  113.9 3.2 %copy-start = (bf16[1,2048,512]{2,1,0:T(8,128)(2,1)S(1)}, bf16[1,2048,512]{2,1,0:T(8,128)(2,1)}, u32[]{:S(2)}) copy-start(bf16[1,2048,512]{2,1,0:T(8,128)(2,1)} %get-tuple-element.9) | copy-start | bytes 6291460
  117.1 1.3 %copy-start.2 = (f32[7,512]{1,0:T(8,128)S(1)}, f32[7,512]{1,0:T(8,128)}, u32[]{:S(2)}) copy-start(f32[7,512]{1,0:T(8,128)} %get-tuple-element.10) | copy-start | bytes 43012
  117.1 1.9 %copy-start.1 = (f32[7,512]{1,0:T(8,128)S(1)}, f32[7,512]{1,0:T(8,128)}, u32[]{:S(2)}) copy-start(f32[7,512]{1,0:T(8,128)} %get-tuple-element.11) | copy-start | bytes 43012

commit v3 on v2

--- a/solution.py
+++ b/solution.py
@@ -19,8 +19,8 @@
     gate_in, value_in, filter_gate, filter_value, teacher_in,
     gate_out, value_out, gate_taps, value_taps,
     raw_g, raw_v, conv_g, conv_v, held, teach, own_n, block_n, total, outgoing, hgrad,
-    out_g, out_v, sums, mine, others,
-    in_sem, out_sem, send_sem, recv_sem, a2a_send, a2a_recv, tap_send, tap_recv,
+    sums, mine, others,
+    in_sem, send_sem, recv_sem, a2a_send, a2a_recv, tap_send, tap_recv,
     near, teach_send_sem, teach_recv_sem,
 ):
     length, width = gate_in.shape[1:]
@@ -326,7 +326,7 @@
             lane = slice(k, min(k + 128, width))
             up = hgrad[pl.ds(base, tile + PAD), lane].astype(f32)
             for b, (conv, raw, weights, store) in enumerate(
-                ((conv_v, raw_g, filter_gate, out_g), (conv_g, raw_v, filter_value, out_v))
+                ((conv_v, raw_g, filter_gate, gate_out), (conv_g, raw_v, filter_value, value_out))
             ):
                 window = up * conv[pl.ds(base, tile + PAD), lane]
                 signal = raw[pl.ds(pl.multiple_of(base + PAD, PAD), tile), lane].astype(f32)
@@ -340,7 +340,7 @@
                     for r in range(8, tile, 8):
                         folded = folded + product[r : r + 8]
                     sums[b, j, :, lane] += folded
-                store[pl.ds(base, tile), lane] = out.astype(bf16)
+                store[0, pl.ds(base, tile), lane] = out.astype(bf16)
 
     tiles = stripe // tile
     per = tiles // pieces
@@ -369,13 +369,6 @@
         return 0
 
     lax.fori_loop(0, groups, last_tiles, 0)
-    out_copies = [
-        pltpu.make_async_copy(src, dst.at[0], out_sem.at[k])
-        for k, (src, dst) in enumerate(((out_g, gate_out), (out_v, value_out)))
-    ]
-    for copy in out_copies:
-        copy.start()
-
     for b in range(2):
         for j in range(taps):
             mine[b, j : j + 1] = jnp.sum(sums[b, j], axis=0, keepdims=True)
@@ -422,8 +415,6 @@
     for target in targets:
         for p in range(pieces):
             exchange(target, p, base_at).wait_send()
-    for copy in out_copies:
-        copy.wait()
 
 
 def on_device(gate_raw, value_raw, filter_gate, filter_value, teacher):
@@ -439,13 +430,13 @@
     return pl.pallas_call(
         functools.partial(kernel, groups, rings, taps, norm_factor),
         out_shape=(
-            jax.ShapeDtypeStruct(gate_raw.shape, bf16),
-            jax.ShapeDtypeStruct(gate_raw.shape, bf16),
+            pltpu.VMEM(gate_raw.shape, bf16),
+            pltpu.VMEM(gate_raw.shape, bf16),
             jax.ShapeDtypeStruct((taps, width), f32),
             jax.ShapeDtypeStruct((taps, width), f32),
         ),
         in_specs=[any_space, any_space, vmem, vmem, any_space],
-        out_specs=(any_space, any_space, vmem, vmem),
+        out_specs=(vmem, vmem, vmem, vmem),
         scratch_shapes=[
             pltpu.VMEM((length + PAD, width), bf16),
             pltpu.VMEM((length + PAD, width), bf16),
@@ -458,13 +449,10 @@
             pltpu.VMEM((stripe, full), f32),
             pltpu.VMEM((groups, stripe, width), bf16),
             pltpu.VMEM((length + PAD, width), bf16),
-            pltpu.VMEM((length, width), bf16),
-            pltpu.VMEM((length, width), bf16),
             pltpu.VMEM((2, taps, 8, width), f32),
             pltpu.VMEM((2, 8, width), f32),
             pltpu.VMEM((rings, 2, 8, width), f32),
             dma((3, groups)),
-            dma((2,)),
             dma((groups, groups)),
             dma((groups, groups)),
             dma((groups, 4)),
@@ -476,7 +464,7 @@
             dma((3,)),
         ],
         compiler_params=pltpu.CompilerParams(
-            collective_id=0, has_side_effects=True, vmem_limit_bytes=60 * 1024 * 1024
+            collective_id=0, has_side_effects=True, vmem_limit_bytes=52 * 1024 * 1024
         ),
     )(gate_raw, value_raw, filter_gate, filter_value, teacher)
 

time: 121 us -> 119 us (0.983)
  local copies, waits for them, and re-layouts: 5.73 us -> 3.86 us
    unnamed x10 -> x8, local copies, waits for them, and re-layouts: 5.73 us -> 3.86 us
where the time goes in v3:
time: 119 us; the launch traced here: 118 us
  Pallas kernels  113 us (95%)
  local copies, waits for them, and re-layouts  3.86 us (3%)
    pallas_call x1, Pallas kernels, on_device(): pl.pallas_call(functools.partial(kernel, groups, rings, taps, norm_factor...  113 us
    unnamed x8, local copies, waits for them, and re-layouts  3.86 us

profile of v3, /device:TPU:0, one launch (start us, length us, event | category | flops | bytes accessed | tf_op | source)
XLA Modules:
  0.0 117.8 jit_solution(3129332646980985734)
XLA Ops:
  0.6 113.3 %shard_map.84 = (bf16[1,2048,512]{2,1,0:T(8,128)(2,1)S(1)}, bf16[1,2048,512]{2,1,0:T(8,128)(2,1)S(1)}, f32[7,512]{1,0:T(8,128)}, f32[7,512]{1,0:T(8,128)}) custom-call(bf16[1,2048,512]{2,1,0:T(8,128)(2,1)} %gate_in.1, bf16[1,2048,512]{2,1,0:T(8,128)(2,1)} %value_in.1, f32[7,512]{1,0:T(8,128)} %filter_gate.1, f32[7,512]{1,0:T(8,128)} %filter_value.1, ...), custom_call_target="tpu_custom_call" | custom-call | tf_op jit(solution)/shard_map/pallas_call | solution.py:430
  113.9 1.3 %copy.13 = bf16[1,2048,512]{2,1,0:T(8,128)(2,1)} copy(bf16[1,2048,512]{2,1,0:T(8,128)(2,1)S(1)} %get-tuple-element.4) | data formatting | bytes 4194304
  115.2 0.0 copy-start.1
  115.2 0.0 copy-start
  115.2 1.3 %copy.14 = bf16[1,2048,512]{2,1,0:T(8,128)(2,1)} copy(bf16[1,2048,512]{2,1,0:T(8,128)(2,1)S(1)} %get-tuple-element.5) | data formatting | bytes 4194304
  116.6 0.0 copy-done.1
  116.6 0.6 copy.15
  117.2 0.0 copy-done
  117.2 0.6 copy.16
Async XLA Ops:
  115.2 1.3 %copy-start.1 = (f32[7,512]{1,0:T(8,128)S(1)}, f32[7,512]{1,0:T(8,128)}, u32[]{:S(2)}) copy-start(f32[7,512]{1,0:T(8,128)} %get-tuple-element.14) | copy-start | bytes 43012
  115.2 1.9 %copy-start = (f32[7,512]{1,0:T(8,128)S(1)}, f32[7,512]{1,0:T(8,128)}, u32[]{:S(2)}) copy-start(f32[7,512]{1,0:T(8,128)} %get-tuple-element.15) | copy-start | bytes 43012
